TPU v7x, 32 devices: a whole 2x2x4 slice. The times are simulated.
32 devices in a mesh: dp: 4 (over y, core), mp: 8 (over z, x).
Axes of the slice: x: 2, y: 2, z: 4, core: 2. Of those that a mesh axis runs over, the one named last changes fastest.
Arguments:
- pair_tokens: bfloat16 [64, 48, 8192], P('dp', None, 'mp'), may hold values from -6 to 6
- norm_gain: float32 [8192], replicated, may hold values from 0.1 to 1.9
- q_weight: bfloat16 [8192, 4096], P('dp', 'mp'), may hold values from -1.5 to 1.5
- k_weight: bfloat16 [8192, 1024], P('dp', 'mp'), may hold values from -1.5 to 1.5
- value_weight: bfloat16 [8192, 1024], P('dp', 'mp'), may hold values from -0.0625 to 0.0625
- o_weight: bfloat16 [4096, 8192], P('mp', 'dp'), may hold values from -0.375 to 0.375
- pair_row: int32 [64], replicated, may hold values from 0 to 15, as said below
- pair_span: int32 [64, 2], replicated, may hold values from 0 to 128, as said below
- block_ids: int32 [2048], P('dp'), may hold values from 0 to 11, as said below
Outputs:
- attn_out: bfloat16 [2048, 8192], P('dp', 'mp')
Inputs may be any that keep to these rules, and one draw needn't show every extreme that they name: `pair_row`: every packed row is tiled exactly by the spans of the pairs that name it; the pairs listed on one index of dp that name rows of one index of dp number at most 4, and 4 is reached. `pair_span`: each span holds one pair, start before end; end - start is at least 3 and at most 48; 48 is reached in every row, and the last pair of every row ends at 128. `block_ids`: the pair's place counts the pairs of its row in order of position; roles are 0 prompt, 1 chosen, 2 rejected, in that order within each pair, each present; consistent with pair_row and pair_span.
All inputs are finite; a program needn't handle non-finite values.
Results may differ from a plain program's by a relative error of at most 0.013.
Values may be sent and summed in bfloat16 or wider, within the bound.
A program may use at most 128 MiB of HBM per device.

v0:
```python
import jax
import jax.numpy as jnp
from jax import lax
from jax.sharding import PartitionSpec as P

HEAD_SIZE = 128
ROW_TOKENS = 128
QUERY_PER_KV = 4


def apply_rotary(values, token_position, heads):
    half = HEAD_SIZE // 2
    freq = 500000.0 ** (-(jnp.arange(half, dtype=jnp.float32) * 2.0 / HEAD_SIZE))
    angle = token_position.astype(jnp.float32)[:, None] * freq[None, :]
    cosine = jnp.cos(angle)[:, None, :]
    sine = jnp.sin(angle)[:, None, :]
    shaped = values.reshape(values.shape[0], heads, HEAD_SIZE)
    first = shaped[..., :half]
    second = shaped[..., half:]
    turned = jnp.concatenate(
        [first * cosine - second * sine, second * cosine + first * sine], axis=-1
    )
    return turned.reshape(values.shape[0], heads * HEAD_SIZE).astype(jnp.bfloat16)


def row_mask(ids):
    pair_of = ids // 3
    role_of = ids % 3
    steps_a = jnp.arange(ids.shape[0])
    causal = steps_a[None, :] <= steps_a[:, None]
    same = pair_of[:, None] == pair_of[None, :]
    hidden_pair = (role_of[:, None] == 2) & (role_of[None, :] == 1)
    return causal & same & jnp.logical_not(hidden_pair)


def local(
    pair_tokens,
    norm_gain,
    q_weight,
    k_weight,
    value_weight,
    o_weight,
    pair_row,
    pair_span,
    block_ids,
):
    dp_count = lax.axis_size("dp")
    own_index = lax.axis_index("dp")
    pairs_dev = pair_tokens.shape[0]
    pair_cap = pair_tokens.shape[1]
    width_local = pair_tokens.shape[2]
    all_pairs = pair_row.shape[0]
    most_sent = -(-pairs_dev // dp_count)
    tok_dev = block_ids.shape[0]
    rows_dev = tok_dev // ROW_TOKENS
    owners_all = (pair_row // rows_dev).reshape(dp_count, pairs_dev)
    same_owner = owners_all[:, :, None] == owners_all[:, None, :]
    listed = jnp.arange(pairs_dev)
    before = listed[None, :] < listed[:, None]
    rank_all = jnp.sum((same_owner & before[None]).astype(jnp.int32), axis=2)
    own_owner = lax.dynamic_index_in_dim(owners_all, own_index, 0, keepdims=False)
    own_rank = lax.dynamic_index_in_dim(rank_all, own_index, 0, keepdims=False)
    outgoing = jnp.zeros((dp_count * most_sent, pair_cap, width_local), jnp.bfloat16)
    outgoing = outgoing.at[own_owner * most_sent + own_rank].set(pair_tokens)
    incoming = lax.all_to_all(
        outgoing.reshape(dp_count, most_sent * pair_cap, width_local),
        "dp",
        split_axis=0,
        concat_axis=0,
        tiled=True,
    )
    slots = jnp.arange(pair_cap, dtype=jnp.int32)
    length = pair_span[:, 1] - pair_span[:, 0]
    source = jnp.arange(all_pairs, dtype=jnp.int32) // pairs_dev
    target = (pair_row % rows_dev)[:, None] * ROW_TOKENS + pair_span[:, 0][:, None] + slots[None, :]
    usable = (owners_all.reshape(-1) == own_index)[:, None] & (slots[None, :] < length[:, None])
    slot_index = (source * most_sent + rank_all.reshape(-1))[:, None] * pair_cap + slots[None, :]
    buffer_size = dp_count * most_sent * pair_cap
    slot_index = jnp.where(usable, slot_index, buffer_size)
    placement_map = jnp.full((buffer_size,), tok_dev, jnp.int32)
    placement_map = placement_map.at[slot_index.reshape(-1)].set(target.reshape(-1), mode="drop")
    packed_local = jnp.zeros((tok_dev, width_local), jnp.bfloat16)
    packed_local = packed_local.at[placement_map].set(
        incoming.reshape(buffer_size, width_local), mode="drop"
    )
    packed = lax.all_gather(packed_local, "mp", axis=1, tiled=True)
    wide = packed.astype(jnp.float32)
    scale = lax.rsqrt(jnp.mean(wide * wide, axis=-1, keepdims=True) + 1e-05)
    normed = (wide * scale * norm_gain[None, :]).astype(jnp.bfloat16)

    def add_rows(piece):
        return jnp.dot(normed, piece, preferred_element_type=jnp.float32)

    query_heads = add_rows(lax.all_gather(q_weight, "dp", axis=0, tiled=True))
    key_rows = add_rows(lax.all_gather(k_weight, "dp", axis=0, tiled=True))
    value_sum = add_rows(lax.all_gather(value_weight, "dp", axis=0, tiled=True))
    value_heads = value_sum.astype(jnp.bfloat16)
    ids_rows = block_ids.reshape(rows_dev, ROW_TOKENS)
    visible = jax.vmap(row_mask)(ids_rows)
    token_position = (jnp.sum(visible.astype(jnp.int32), axis=2) - 1).reshape(tok_dev)
    kv_local = k_weight.shape[1] // HEAD_SIZE
    q_local = q_weight.shape[1] // HEAD_SIZE
    rotated_query = apply_rotary(query_heads, token_position, q_local).reshape(
        rows_dev, ROW_TOKENS, kv_local, QUERY_PER_KV, HEAD_SIZE
    )
    rotated_key = apply_rotary(key_rows, token_position, kv_local).reshape(
        rows_dev, ROW_TOKENS, kv_local, HEAD_SIZE
    )
    v_rows = value_heads.reshape(rows_dev, ROW_TOKENS, kv_local, HEAD_SIZE)
    scores = jnp.einsum(
        "rihgd,rjhd->rhgij", rotated_query, rotated_key, preferred_element_type=jnp.float32
    ) * HEAD_SIZE ** (-0.5)
    scores = jnp.where(visible[:, None, None], scores, -1e30)
    top = jnp.max(scores, axis=-1, keepdims=True)
    expo = jnp.exp(scores - top)
    probs = (expo / jnp.sum(expo, axis=-1, keepdims=True)).astype(jnp.bfloat16)
    attn = jnp.einsum(
        "rhgij,rjhd->rihgd", probs, v_rows, preferred_element_type=jnp.float32
    ).astype(jnp.bfloat16)
    attn = attn.reshape(tok_dev, q_local * HEAD_SIZE)
    terms = jnp.dot(
        attn, lax.all_gather(o_weight, "dp", axis=1, tiled=True), preferred_element_type=jnp.float32
    )
    return lax.psum_scatter(terms.astype(jnp.bfloat16), "mp", scatter_dimension=1, tiled=True)


def solution(mesh):
    placed = (
        P("dp", None, "mp"),
        P(),
        P("dp", "mp"),
        P("dp", "mp"),
        P("dp", "mp"),
        P("mp", "dp"),
        P(),
        P(),
        P("dp"),
    )
    return jax.shard_map(
        local, mesh=mesh, in_specs=placed, out_specs=P("dp", "mp"), check_vma=False
    )
```

profile of v0, /device:TPU:17, one launch (start us, length us, event | category | flops | bytes accessed | tf_op | source)
XLA Modules:
  0.0 499.4 jit_solution(16550077983021786801)
XLA Ops:
  6.6 0.7 broadcast_compare_fusion.2
  7.3 0.1 eq.64
  7.4 0.2 convert_reduce_fusion.1
  7.6 1.3 broadcast_in_dim.24
  8.9 5.4 %scatter_fusion = bf16[16,48,1024]{2,1,0:T(8,128)(2,1)} fusion(bf16[16,48,1024]{2,1,0:T(8,128)(2,1)} %broadcast_in_dim.24, s32[16]{0:T(128)S(1)} %fusion.33, bf16[16,48,1024]{2,1,0:T(8,128)(2,1)} %param.9), kind=kCustom, calls=%fused_computation.1 | custom fusion | bytes 4718656 | tf_op jit(solution)/shard_map/scatter | solution.py:64
  14.4 4.2 all-to-all-start
  18.6 0.1 reshape.394
  18.7 0.1 add_select_fusion
  18.8 0.1 select_n.97
  18.9 0.1 iota_add_fusion
  18.9 0.1 reshape.406
  19.0 11.8 %scatter_custom_fusion = s32[768]{0:T(1024)S(1)} fusion(s32[3072]{0:T(1024)S(1)} %bitcast.87, s32[3072]{0:T(1024)S(1)} %reshape.406, s32[]{:T(128)} %constant.90.clone.1), kind=kCustom, calls=%fused_computation.60 | custom fusion | bytes 3076 | tf_op jit(solution)/shard_map/scatter | solution.py:81
  30.8 6.8 %all-to-all-done = bf16[4,192,1024]{2,1,0:T(8,128)(2,1)S(1)} async-done(((bf16[4,192,1024]{2,1,0:T(8,128)(2,1)}), bf16[4,192,1024]{2,1,0:T(8,128)(2,1)S(1)}, u32[]{:S(2)}, u32[]{:S(2)}) %all-to-all-start) | async-done | bytes 1572896 | tf_op jit(solution)/shard_map/all_to_all | solution.py:65
  37.6 6.7 %scatter_custom_fusion.2 = bf16[512,1024]{1,0:T(8,128)(2,1)} fusion(s32[768]{0:T(1024)S(1)} %compare_select_fusion.1, bf16[768,1024]{1,0:T(8,128)(2,1)S(1)} %bitcast.83, bf16[]{:T(256)} %constant.89.clone.1), kind=kCustom, calls=%fused_computation.26 | custom fusion | bytes 1048578 | tf_op jit(solution)/shard_map/scatter | solution.py:83
  44.3 0.0 all-gather.6.cloned.1.call-update
  44.3 0.0 all-gather.12.cloned.1.call-start
  44.4 0.7 all-gather.12.cloned.1.call-update
  45.1 0.0 all-gather.10.cloned.1.call-start
  45.1 0.7 all-gather.10.cloned.1.call-update
  45.8 0.0 all-gather.8.cloned.1.call-start
  45.9 0.5 all-gather.8.cloned.1.call-update
  46.4 0.0 all-gather.14.cloned.1.call-start
  46.4 0.5 all-gather.14.cloned.1.call-update
  47.0 0.0 reduce-scatter.2.cloned.1.call-start
  47.1 0.2 convert_reduce_fusion
  47.3 1.0 multiply_cosine_fusion
  48.3 119.4 %all-gather.6.cloned.1.call-done = bf16[512,8192]{1,0:T(8,128)(2,1)} async-done(((bf16[512,1024]{1,0:T(8,128)(2,1)}), bf16[512,8192]{1,0:T(8,128)(2,1)}) %all-gather.6.cloned.1.call-update) | async-done | bytes 8388624 | tf_op jit(solution)/shard_map/all_gather | solution.py:86
  167.7 5.1 %fusion = f32[512]{0:T(512)S(1)} fusion(bf16[512,8192]{1,0:T(8,128)(2,1)} %all-gather.6.cloned.1.call-done), kind=kLoop, calls=%fused_computation.5 | loop fusion | flops 12582400 | bytes 8390656 | tf_op jit(solution)/shard_map/reduce_sum | solution.py:88
  172.8 55.0 %all-gather.12.cloned.1.call-done = bf16[8192,512]{1,0:T(8,128)(2,1)} async-done(((bf16[2048,512]{1,0:T(8,128)(2,1)}), bf16[8192,512]{1,0:T(8,128)(2,1)}) %all-gather.12.cloned.1.call-update) | async-done | bytes 8388624 | tf_op jit(solution)/shard_map/all_gather | solution.py:94
  227.8 11.4 %fusion.35 = f32[512,512]{0,1:T(8,128)S(1)} fusion(bf16[8192,512]{1,0:T(8,128)(2,1)} %all-gather.12.cloned.1.call-done, bf16[512,8192]{1,0:T(8,128)(2,1)} %all-gather.6.cloned.1.call-done, f32[8192]{0:T(1024)S(1)} %copy-done.3, f32[512]{0:T(512)S(1)} %add_rsqrt_fusion), kind=kOutput, calls=%fused_computation.87 | convolution fusion | flops 4311744512 | bytes 17860608 | tf_op jit(solution)/shard_map/dot_general | solution.py:92
  239.2 0.1 fusion.39
  239.3 0.3 copy.33
  239.6 0.3 copy.34
  239.9 12.0 %all-gather.10.cloned.1.call-done = bf16[8192,128]{1,0:T(8,128)(2,1)} async-done(((bf16[2048,128]{1,0:T(8,128)(2,1)}), bf16[8192,128]{1,0:T(8,128)(2,1)}) %all-gather.10.cloned.1.call-update) | async-done | bytes 2097168 | tf_op jit(solution)/shard_map/all_gather | solution.py:95
  251.9 6.5 %convolution_bitcast_fusion = f32[512,1,128]{0,2,1:T(8,128)S(1)} fusion(bf16[8192,128]{1,0:T(8,128)(2,1)} %all-gather.10.cloned.1.call-done, bf16[512,8192]{1,0:T(8,128)(2,1)} %all-gather.6.cloned.1.call-done, f32[8192]{0:T(1024)S(1)} %copy-done.3, f32[512]{0:T(512)S(1)} %add_rsqrt_fusion), kind=kOutput, calls=%fused_computation.14 | convolution fusion | flops 1090519040 | bytes 10782720 | tf_op jit(solution)/shard_map/dot_general | solution.py:92
  258.4 0.6 fusion.18
  259.0 0.1 copy.32
  259.1 0.3 subtract_convert_fusion
  259.4 0.3 pad_maximum_fusion
  259.7 0.3 fusion.40
  260.1 0.2 fusion.6
  260.2 15.7 %all-gather.8.cloned.1.call-done = bf16[8192,128]{1,0:T(8,128)(2,1)} async-done(((bf16[2048,128]{1,0:T(8,128)(2,1)}), bf16[8192,128]{1,0:T(8,128)(2,1)}) %all-gather.8.cloned.1.call-update) | async-done | bytes 2097168 | tf_op jit(solution)/shard_map/all_gather | solution.py:96
  276.0 6.4 %convolution_convert_fusion.2 = bf16[512,128]{1,0:T(8,128)(2,1)S(1)} fusion(bf16[8192,128]{1,0:T(8,128)(2,1)} %all-gather.8.cloned.1.call-done, bf16[512,8192]{1,0:T(8,128)(2,1)} %all-gather.6.cloned.1.call-done, f32[8192]{0:T(1024)S(1)} %copy-done.3, f32[512]{0:T(512)S(1)} %add_rsqrt_fusion), kind=kOutput, calls=%fused_computation.15 | convolution fusion | flops 1090584576 | bytes 10651648 | tf_op jit(solution)/shard_map/dot_general | solution.py:92
  282.3 0.4 fusion.5
  282.7 0.3 copy.26
  283.0 52.7 %all-gather.14.cloned.1.call-done = bf16[512,8192]{1,0:T(8,128)(2,1)} async-done(((bf16[512,2048]{1,0:T(8,128)(2,1)}), bf16[512,8192]{1,0:T(8,128)(2,1)}) %all-gather.14.cloned.1.call-update) | async-done | bytes 8388624 | tf_op jit(solution)/shard_map/all_gather | solution.py:122
  335.7 10.1 %convolution_convert_fusion = bf16[512,8192]{1,0:T(8,128)(2,1)} fusion(bf16[512,8192]{1,0:T(8,128)(2,1)} %all-gather.14.cloned.1.call-done, bf16[64,8,4,128]{3,2,1,0:T(4,128)(2,1)S(1)} %bitcast.86), kind=kOutput, calls=%fused_computation.8 | convolution fusion | flops 4299161600 | bytes 17301504 | tf_op jit(solution)/shard_map/dot_general | solution.py:121
  345.9 146.7 %reduce-scatter.2.cloned.1.call-done = bf16[512,1024]{1,0:T(8,128)(2,1)} async-done(((bf16[512,8192]{1,0:T(8,128)(2,1)}), bf16[512,1024]{1,0:T(8,128)(2,1)}) %reduce-scatter.2.cloned.1.call-update) | async-done | bytes 1048592 | tf_op jit(solution)/shard_map/reduce_scatter | solution.py:124
  (23 shorter events, 0.2 us)
Async XLA Ops:
  6.5 12.1 %copy-start.1 = (s32[64]{0:T(128)S(1)}, s32[64]{0:T(128)}, u32[]{:S(2)}) copy-start(s32[64]{0:T(128)} %param.15) | copy-start | bytes 772
  6.5 12.1 %copy-start.2 = (s32[64,2]{0,1:T(2,128)S(1)}, s32[64,2]{0,1:T(2,128)}, u32[]{:S(2)}) copy-start(s32[64,2]{0,1:T(2,128)} %param.16) | copy-start | bytes 1540
  7.6 39.5 %copy-start = (s32[512]{0:T(512)S(1)}, s32[512]{0:T(512)}, u32[]{:S(2)}) copy-start(s32[512]{0:T(512)} %param.17) | copy-start | bytes 6148
  14.4 23.3 %all-to-all-start = ((bf16[4,192,1024]{2,1,0:T(8,128)(2,1)}), bf16[4,192,1024]{2,1,0:T(8,128)(2,1)S(1)}, u32[]{:S(2)}, u32[]{:S(2)}) async-start(bf16[4,192,1024]{2,1,0:T(8,128)(2,1)} %bitcast.6), calls=%async_computation | async-start | bytes 3145728 | tf_op jit(solution)/shard_map/all_to_all | solution.py:65
  18.6 209.2 %copy-start.3 = (f32[8192]{0:T(1024)S(1)}, f32[8192]{0:T(1024)}, u32[]{:S(2)}) copy-start(f32[8192]{0:T(1024)} %param.10) | copy-start | bytes 98308
  18.6 149.2 %all-gather.6.cloned.1.call-start = ((), (), s32[]{:S(2)}) async-start(), calls=%async_computation.2 | async-start | bytes 9437184 | tf_op jit(solution)/shard_map/all_gather | solution.py:86
  44.3 183.5 %all-gather.12.cloned.1.call-start = ((), (), s32[]{:S(2)}) async-start(), calls=%async_computation.5 | async-start | bytes 10485760 | tf_op jit(solution)/shard_map/all_gather | solution.py:94
  45.1 206.9 %all-gather.10.cloned.1.call-start = ((), (), s32[]{:S(2)}) async-start(), calls=%async_computation.4 | async-start | bytes 2621440 | tf_op jit(solution)/shard_map/all_gather | solution.py:95
  45.8 230.1 %all-gather.8.cloned.1.call-start = ((), (), s32[]{:S(2)}) async-start(), calls=%async_computation.3 | async-start | bytes 2621440 | tf_op jit(solution)/shard_map/all_gather | solution.py:96
  46.4 289.4 %all-gather.14.cloned.1.call-start = ((), (), s32[]{:S(2)}) async-start(), calls=%async_computation.6 | async-start | bytes 10485760 | tf_op jit(solution)/shard_map/all_gather | solution.py:122
  47.0 445.5 %reduce-scatter.2.cloned.1.call-start = ((), (), s32[]{:S(2)}) async-start(), calls=%async_computation.7 | async-start | bytes 9437184 | tf_op jit(solution)/shard_map/reduce_scatter | solution.py:124
Sparse Core Ops, SparseCore 0:
  44.5 123.2 all-gather.5
  169.3 58.4 all-gather.11
  229.4 22.5 all-gather.9
  253.4 22.5 all-gather.7
  277.4 58.3 all-gather.13
  346.0 146.4 reduce-scatter.1
where the time goes:
time: 502 us; the launch traced here: 499 us
  waiting for transfers between devices  411 us (82%)
  matrix products  35 us (7%)
  local copies, waits for them, and re-layouts  26.7 us (5%)
  between operations  13.7 us (3%)
  other arithmetic  8.88 us (2%)
    reduce_scatter x1, waiting for transfers between devices, local(): lax.psum_scatter(terms.astype(jnp.bfloat16), 'mp', scatter_dimension=1, t...  147 us
    all_gather x1, waiting for transfers between devices, local(): packed = lax.all_gather(packed_local, 'mp', axis=1, tiled=True)  119 us
    all_gather x1, waiting for transfers between devices, local(): query_heads = add_rows(lax.all_gather(q_weight, 'dp', axis=0, tiled=True))  55 us
    all_gather x1, waiting for transfers between devices, local(): lax.all_gather(o_weight, 'dp', axis=1, tiled=True)  52.7 us
    dot_general x3, matrix products, add_rows(): return jnp.dot(normed, piece, preferred_element_type=jnp.float32)  24.2 us
    all_gather x1, waiting for transfers between devices, local(): value_sum = add_rows(lax.all_gather(value_weight, 'dp', axis=0, tiled=True))  15.7 us
    all_gather x1, waiting for transfers between devices, local(): key_rows = add_rows(lax.all_gather(k_weight, 'dp', axis=0, tiled=True))  12 us
    scatter x1, local copies, waits for them, and re-layouts, local(): placement_map.at[slot_index.reshape(-1)]  11.8 us
  transfers between devices with their start and end apart: 7, of which 7 were waited for; matrix products, arithmetic and copies ran while one was open for 9% of the time, Pallas kernels for 0%

commit v1 on v0

v1 whole, which is shorter than its diff:
```python
import functools

import jax
import jax.numpy as jnp
from jax import lax
from jax.experimental import pallas as pl
from jax.experimental.pallas import tpu as pltpu
from jax.sharding import PartitionSpec as P

HEAD_SIZE = 128
ROW_TOKENS = 128
QUERY_PER_KV = 4
PIECES = 2
MESH = pl.DeviceIdType.MESH


def row_mask(ids):
    pair_of = ids // 3
    role_of = ids % 3
    steps_a = jnp.arange(ids.shape[0])
    causal = steps_a[None, :] <= steps_a[:, None]
    same = pair_of[:, None] == pair_of[None, :]
    hidden_pair = (role_of[:, None] == 2) & (role_of[None, :] == 1)
    return causal & same & jnp.logical_not(hidden_pair)


def ring_member(place, count):
    place = lax.rem(place + 2 * count, count)
    return jnp.where(place < count // 2, 2 * place, 2 * (count - 1 - place) + 1)


def kernel(
    n_dp, n_mp,
    x_ref, gain_ref, q_ref, k_ref, v_ref, o_ref, cos_ref, sin_ref, vis_ref,
    out_ref,
    xg, wq, wk, wv, wo, acc, attn, sums, terms,
    own_sem, w_send, w_recv, x_send, x_recv, s_send, s_recv,
):
    me_dp = lax.axis_index("dp")
    me_mp = lax.axis_index("mp")
    place = jnp.where(lax.rem(me_mp, 2) == 0, me_mp // 2, n_mp - 1 - me_mp // 2)
    sides = (ring_member(place + 1, n_mp), ring_member(place - 1, n_mp))
    groups = n_dp // 2
    core = lax.rem(me_dp, 2)
    partner = me_dp + 1 - 2 * core
    others = [lax.rem(me_dp + 2 * j, n_dp) for j in range(1, groups)]
    tokens, chunk = x_ref.shape
    half = tokens // 2
    piece = half // PIECES

    barrier = pltpu.get_barrier_semaphore()
    for side in sides:
        pl.semaphore_signal(barrier, inc=1, device_id={"mp": side}, device_id_type=MESH)
    for peer in [partner] + others:
        pl.semaphore_signal(barrier, inc=1, device_id={"dp": peer}, device_id_type=MESH)
    pl.semaphore_wait(barrier, 2 + 1 + len(others))

    def part(which, owner):
        if which == 3:
            width = o_ref.shape[1]
            return wo.at[:, pl.ds(pl.multiple_of(owner * width, 128), width)]
        full = (wq, wk, wv)[which]
        depth = q_ref.shape[0]
        return full.at[pl.ds(pl.multiple_of(owner * depth, 16), depth), :]

    shards = (q_ref, k_ref, v_ref, o_ref)

    def weight_copy(which, owner, source, slot, peer):
        return pltpu.make_async_remote_copy(
            src_ref=source,
            dst_ref=part(which, owner),
            send_sem=w_send.at[which, slot],
            recv_sem=w_recv.at[which, owner],
            device_id={"dp": peer},
            device_id_type=MESH,
        )

    def x_copy(step, way, sub):
        sign = -1 if way == 0 else 1
        chunk_of = ring_member(place + sign * step, n_mp)
        rows = pl.ds(way * half + sub * piece, piece)
        ref = xg.at[chunk_of, rows, :]
        return pltpu.make_async_remote_copy(
            src_ref=ref,
            dst_ref=ref,
            send_sem=x_send.at[way, sub, step],
            recv_sem=x_recv.at[way, sub, step],
            device_id={"mp": sides[way]},
            device_id_type=MESH,
        )

    def x_arrival(step, way, sub):
        sign = -1 if way == 0 else 1
        chunk_of = ring_member(place + sign * (step + 1), n_mp)
        rows = pl.ds(way * half + sub * piece, piece)
        ref = xg.at[chunk_of, rows, :]
        return pltpu.make_async_remote_copy(
            src_ref=ref,
            dst_ref=ref,
            send_sem=x_send.at[way, sub, step],
            recv_sem=x_recv.at[way, sub, step],
            device_id={"mp": sides[way]},
            device_id_type=MESH,
        )

    own_x = pltpu.make_async_copy(x_ref, xg.at[me_mp], own_sem.at[4])
    own_x.start()
    owns = [
        pltpu.make_async_copy(shards[w], part(w, me_dp), own_sem.at[w]) for w in range(4)
    ]
    for w in range(4):
        for j, peer in enumerate(others):
            weight_copy(w, me_dp, shards[w], 1 + j, peer).start()
    own_x.wait()
    for sub in range(PIECES):
        for way in range(2):
            x_copy(0, way, sub).start()
    for w in range(4):
        owns[w].start()
        weight_copy(w, me_dp, shards[w], 0, partner).start()

    def pass_weight(w):
        for j in range(1, groups):
            owner = lax.rem(me_dp + n_dp - 2 * j, n_dp)
            weight_copy(w, owner, part(w, owner), 0, partner).wait_recv()
            weight_copy(w, owner, part(w, owner), groups + j - 1, partner).start()

    def weight_done(w):
        owns[w].wait()
        for i in range(groups):
            owner = lax.rem(partner + 2 * i, n_dp)
            weight_copy(w, owner, part(w, owner), 0, partner).wait_recv()

    def gather_step(step, carry):
        for sub in range(PIECES):
            for way in range(2):
                x_arrival(step, way, sub).wait_recv()
                x_copy(step + 1, way, sub).start()
        return carry

    late = max(n_mp - 3, 0)
    lax.fori_loop(0, late, gather_step, 0)
    pass_weight(0)
    lax.fori_loop(late, n_mp - 2, gather_step, 0)
    pass_weight(1)
    pass_weight(2)
    for sub in range(PIECES):
        for way in range(2):
            x_arrival(n_mp - 2, way, sub).wait_recv()
    for w in range(3):
        weight_done(w)

    q_width = wq.shape[1]
    k_width = wk.shape[1]
    acc[...] = jnp.zeros_like(acc)

    def project(g, squares):
        wide = xg[g].astype(jnp.float32)
        squares = squares + jnp.sum(wide * wide, axis=1, keepdims=True)
        scaled = (wide * gain_ref[pl.ds(g, 1), :]).astype(jnp.bfloat16)
        rows = pl.ds(pl.multiple_of(g * chunk, 16), chunk)
        acc[:, 0:q_width] += jnp.dot(scaled, wq[rows, :], preferred_element_type=jnp.float32)
        acc[:, q_width:q_width + k_width] += jnp.dot(
            scaled, wk[rows, :], preferred_element_type=jnp.float32
        )
        acc[:, q_width + k_width:] += jnp.dot(
            scaled, wv[rows, :], preferred_element_type=jnp.float32
        )
        return squares

    squares = lax.fori_loop(0, n_mp, project, jnp.zeros((tokens, 1), jnp.float32))
    acc[...] = acc[...] * lax.rsqrt(squares / (n_mp * chunk) + 1e-05)

    def turn(u, cosine, sine):
        return (u * cosine + pltpu.roll(u, HEAD_SIZE // 2, 1) * sine).astype(jnp.bfloat16)

    def attend(r, carry):
        rows = pl.ds(pl.multiple_of(r * ROW_TOKENS, ROW_TOKENS), ROW_TOKENS)
        cosine = cos_ref[rows, :]
        sine = sin_ref[rows, :]
        seen = vis_ref[rows, :] > 0
        for kv in range(k_width // HEAD_SIZE):
            at_k = q_width + kv * HEAD_SIZE
            key = turn(acc[rows, at_k:at_k + HEAD_SIZE], cosine, sine)
            value = acc[rows, at_k + k_width:at_k + k_width + HEAD_SIZE].astype(jnp.bfloat16)
            for h in range(kv * QUERY_PER_KV, (kv + 1) * QUERY_PER_KV):
                at = slice(h * HEAD_SIZE, (h + 1) * HEAD_SIZE)
                query = turn(acc[rows, at], cosine, sine)
                scores = lax.dot_general(
                    query, key, (((1,), (1,)), ((), ())), preferred_element_type=jnp.float32
                ) * HEAD_SIZE ** (-0.5)
                scores = jnp.where(seen, scores, -1e30)
                expo = jnp.exp(scores - jnp.max(scores, axis=-1, keepdims=True))
                probs = (expo / jnp.sum(expo, axis=-1, keepdims=True)).astype(jnp.bfloat16)
                attn[rows, at] = jnp.dot(
                    probs, value, preferred_element_type=jnp.float32
                ).astype(jnp.bfloat16)
        return carry

    lax.fori_loop(0, tokens // ROW_TOKENS, attend, 0)
    pass_weight(3)
    weight_done(3)

    def make_terms(hop):
        for way in range(2):
            sign = -1 if way == 0 else 1
            g = ring_member(place + sign * hop, n_mp)
            columns = pl.ds(pl.multiple_of(g * chunk, 128), chunk)
            terms[way] = jnp.dot(
                attn[way * half:(way + 1) * half, :],
                wo[:, columns],
                preferred_element_type=jnp.float32,
            )

    def sum_copy(slot, way, sub):
        rows = pl.ds(sub * piece, piece)
        return pltpu.make_async_remote_copy(
            src_ref=sums.at[way, slot, rows, :],
            dst_ref=sums.at[way, slot + 1, rows, :],
            send_sem=s_send.at[way, sub, slot],
            recv_sem=s_recv.at[way, sub, slot],
            device_id={"mp": sides[way]},
            device_id_type=MESH,
        )

    make_terms(1)
    for sub in range(PIECES):
        for way in range(2):
            rows = slice(sub * piece, (sub + 1) * piece)
            sums[way, 0, rows, :] = terms[way, rows, :].astype(jnp.bfloat16)
            sum_copy(0, way, sub).start()

    def scatter_step(step, carry):
        make_terms(step + 2)
        for sub in range(PIECES):
            for way in range(2):
                sum_copy(step, way, sub).wait_recv()
                rows = slice(sub * piece, (sub + 1) * piece)
                total = sums[way, step + 1, rows, :].astype(jnp.float32) + terms[way, rows, :]
                sums[way, step + 1, rows, :] = total.astype(jnp.bfloat16)
                sum_copy(step + 1, way, sub).start()
        return carry

    lax.fori_loop(0, n_mp - 2, scatter_step, 0)
    make_terms(n_mp)
    for sub in range(PIECES):
        for way in range(2):
            sum_copy(n_mp - 2, way, sub).wait_recv()
            rows = slice(sub * piece, (sub + 1) * piece)
            total = sums[way, n_mp - 1, rows, :].astype(jnp.float32) + terms[way, rows, :]
            start = way * half + sub * piece
            out_ref[start:start + piece, :] = total.astype(jnp.bfloat16)

    def drain(step, carry):
        for sub in range(PIECES):
            for way in range(2):
                x_copy(step, way, sub).wait_send()
                sum_copy(step, way, sub).wait_send()
        return carry

    lax.fori_loop(0, n_mp - 1, drain, 0)
    for w in range(4):
        for i in range(2 * groups - 1):
            weight_copy(w, me_dp, shards[w], i, partner).wait_send()


def local(
    pair_tokens,
    norm_gain,
    q_weight,
    k_weight,
    value_weight,
    o_weight,
    pair_row,
    pair_span,
    block_ids,
):
    dp_count = lax.axis_size("dp")
    mp_count = lax.axis_size("mp")
    own_index = lax.axis_index("dp")
    pairs_dev = pair_tokens.shape[0]
    pair_cap = pair_tokens.shape[1]
    width_local = pair_tokens.shape[2]
    all_pairs = pair_row.shape[0]
    most_sent = -(-pairs_dev // dp_count)
    tok_dev = block_ids.shape[0]
    rows_dev = tok_dev // ROW_TOKENS
    owners_all = (pair_row // rows_dev).reshape(dp_count, pairs_dev)
    same_owner = owners_all[:, :, None] == owners_all[:, None, :]
    listed = jnp.arange(pairs_dev)
    before = listed[None, :] < listed[:, None]
    rank_all = jnp.sum((same_owner & before[None]).astype(jnp.int32), axis=2)
    own_owner = lax.dynamic_index_in_dim(owners_all, own_index, 0, keepdims=False)
    own_rank = lax.dynamic_index_in_dim(rank_all, own_index, 0, keepdims=False)
    slots = jnp.arange(pair_cap, dtype=jnp.int32)
    sent = dp_count * most_sent
    own_slot = ((own_owner * most_sent + own_rank)[:, None] * pair_cap + slots[None, :]).reshape(-1)
    pick = (jnp.arange(sent * pair_cap)[:, None] == own_slot[None, :]).astype(jnp.bfloat16)
    outgoing = jnp.dot(
        pick,
        pair_tokens.reshape(pairs_dev * pair_cap, width_local),
        preferred_element_type=jnp.float32,
    ).astype(jnp.bfloat16)
    incoming = lax.all_to_all(
        outgoing.reshape(dp_count, most_sent * pair_cap, width_local),
        "dp",
        split_axis=0,
        concat_axis=0,
        tiled=True,
    )
    length = pair_span[:, 1] - pair_span[:, 0]
    source = jnp.arange(all_pairs, dtype=jnp.int32) // pairs_dev
    first = (pair_row % rows_dev) * ROW_TOKENS + pair_span[:, 0]
    place = source * most_sent + rank_all.reshape(-1)
    mine = owners_all.reshape(-1) == own_index
    match = (jnp.arange(sent)[:, None] == place[None, :]) & mine[None, :]
    first_of = jnp.sum(jnp.where(match, first[None, :], 0), axis=1)
    length_of = jnp.sum(jnp.where(match, length[None, :], 0), axis=1)
    placement_map = jnp.where(
        slots[None, :] < length_of[:, None], first_of[:, None] + slots[None, :], tok_dev
    ).reshape(-1)
    put = (jnp.arange(tok_dev)[:, None] == placement_map[None, :]).astype(jnp.bfloat16)
    packed_local = jnp.dot(
        put,
        incoming.reshape(sent * pair_cap, width_local),
        preferred_element_type=jnp.float32,
    ).astype(jnp.bfloat16)

    ids_rows = block_ids.reshape(rows_dev, ROW_TOKENS)
    visible = jax.vmap(row_mask)(ids_rows)
    token_position = (jnp.sum(visible.astype(jnp.int32), axis=2) - 1).reshape(tok_dev)
    half = HEAD_SIZE // 2
    freq = 500000.0 ** (-(jnp.arange(half, dtype=jnp.float32) * 2.0 / HEAD_SIZE))
    angle = token_position.astype(jnp.float32)[:, None] * freq[None, :]
    cosine = jnp.cos(angle)
    sine = jnp.sin(angle)
    cosine = jnp.concatenate([cosine, cosine], axis=1)
    sine = jnp.concatenate([-sine, sine], axis=1)
    seen = visible.astype(jnp.int32).reshape(tok_dev, ROW_TOKENS)

    q_width = q_weight.shape[1]
    k_width = k_weight.shape[1]
    width = norm_gain.shape[0]
    far = dp_count - 1
    vmem = pl.BlockSpec(memory_space=pltpu.VMEM)
    anyspace = pl.BlockSpec(memory_space=pl.ANY)
    bf16 = jnp.bfloat16
    return pl.pallas_call(
        functools.partial(kernel, dp_count, mp_count),
        out_shape=jax.ShapeDtypeStruct((tok_dev, width_local), bf16),
        in_specs=[anyspace, vmem, anyspace, anyspace, anyspace, anyspace, vmem, vmem, vmem],
        out_specs=vmem,
        scratch_shapes=[
            pltpu.VMEM((mp_count, tok_dev, width_local), bf16),
            pltpu.VMEM((width, q_width), bf16),
            pltpu.VMEM((width, k_width), bf16),
            pltpu.VMEM((width, k_width), bf16),
            pltpu.VMEM((o_weight.shape[0], width), bf16),
            pltpu.VMEM((tok_dev, q_width + 2 * k_width), jnp.float32),
            pltpu.VMEM((tok_dev, q_width), bf16),
            pltpu.VMEM((2, mp_count, tok_dev // 2, width_local), bf16),
            pltpu.VMEM((2, tok_dev // 2, width_local), jnp.float32),
            pltpu.SemaphoreType.DMA((5,)),
            pltpu.SemaphoreType.DMA((4, far)),
            pltpu.SemaphoreType.DMA((4, dp_count)),
            pltpu.SemaphoreType.DMA((2, PIECES, mp_count - 1)),
            pltpu.SemaphoreType.DMA((2, PIECES, mp_count - 1)),
            pltpu.SemaphoreType.DMA((2, PIECES, mp_count - 1)),
            pltpu.SemaphoreType.DMA((2, PIECES, mp_count - 1)),
        ],
        compiler_params=pltpu.CompilerParams(
            collective_id=0, has_side_effects=True, vmem_limit_bytes=60 * 1024 * 1024
        ),
    )(
        packed_local,
        norm_gain.reshape(mp_count, width_local),
        q_weight,
        k_weight,
        value_weight,
        o_weight,
        cosine,
        sine,
        seen,
    )


def solution(mesh):
    placed = (
        P("dp", None, "mp"),
        P(),
        P("dp", "mp"),
        P("dp", "mp"),
        P("dp", "mp"),
        P("mp", "dp"),
        P(),
        P(),
        P("dp"),
    )
    return jax.shard_map(
        local, mesh=mesh, in_specs=placed, out_specs=P("dp", "mp"), check_vma=False
    )
```

time: 502 us -> 237 us (0.47)
  waiting for transfers between devices: 411 us -> 14.7 us
  Pallas kernels: 0 us -> 204 us
  matrix products: 35 us -> 4.5 us
  local copies, waits for them, and re-layouts: 26.7 us -> 3.38 us
  between operations: 13.7 us -> 0.08 us
    all_gather x5 -> x0, waiting for transfers between devices: 255 us -> none  [the longest x1 119 us: local(): packed = lax.all_gather(packed_local, 'mp', axis=1, tiled=True)]
    pallas_call x0 -> x1, Pallas kernels: none -> 204 us  [local(): pl.pallas_call(functools.partial(kernel, dp_count, mp_count), out_shape=j...]
    reduce_scatter x1 -> x0, waiting for transfers between devices: 147 us -> none  [local(): lax.psum_scatter(terms.astype(jnp.bfloat16), 'mp', scatter_dimension=1, t...]
    dot_general x6 -> x2, matrix products: 35 us -> 4.5 us  [the longest x1 2.55 us: local(): jnp.dot(pick, pair_tokens.reshape(pairs_dev * pair_cap, width_local), pre...]
    scatter x3 -> x0, local copies, waits for them, and re-layouts: 23.9 us -> none  [the longest x1 11.8 us: local(): placement_map.at[slot_index.reshape(-1)]]
    all_to_all x1, waiting for transfers between devices: 6.8 us -> 14.7 us  [local(): lax.all_to_all(outgoing.reshape(dp_count, most_sent * pair_cap, width_loc...]
    reduce_sum x2 -> x1, other arithmetic: 5.27 us -> 0.12 us  [local(): length_of = jnp.sum(jnp.where(match, length[None, :], 0), axis=1)]
  transfers between devices with their start and end apart: 7 -> 1, of which waited for: 7 -> 1; matrix products, arithmetic and copies ran while one was open for 9% -> 2% of each run, Pallas kernels for 0% -> 0%
where the time goes in v1:
time: 237 us; the launch traced here: 235 us
  Pallas kernels  204 us (86%)
  waiting for transfers between devices  14.7 us (6%)
  other arithmetic  4.65 us (2%)
  matrix products  4.5 us (2%)
  starting transfers between devices  4.35 us (2%)
  local copies, waits for them, and re-layouts  3.38 us (1%)
    pallas_call x1, Pallas kernels, local(): pl.pallas_call(functools.partial(kernel, dp_count, mp_count), out_shape=j...  204 us
    all_to_all x1, waiting for transfers between devices, local(): lax.all_to_all(outgoing.reshape(dp_count, most_sent * pair_cap, width_loc...  14.7 us
  transfers between devices with their start and end apart: 1, of which 1 were waited for; matrix products, arithmetic and copies ran while one was open for 2% of the time, Pallas kernels for 0%

profile of v1, /device:TPU:17, one launch (start us, length us, event | category | flops | bytes accessed | tf_op | source)
XLA Modules:
  0.0 235.5 jit_solution(9267380659866591774)
XLA Ops:
  0.0 0.0 copy-start
  0.0 0.8 broadcast_compare_fusion.2
  0.8 0.1 eq.111
  0.9 0.2 convert_reduce_fusion.1
  1.1 0.1 iota_add_fusion
  1.2 0.1 add.112
  1.3 0.2 copy-done
  1.4 2.5 %fusion.1 = bf16[768,1024]{1,0:T(8,128)(2,1)} fusion(bf16[768,1024]{1,0:T(8,128)(2,1)S(1)} %bitcast.52, s32[768]{0:T(1024)S(1)} %add.112), kind=kOutput, calls=%fused_computation.2 | convolution fusion | flops 1209335808 | bytes 3148800 | tf_op jit(solution)/shard_map/dot_general | solution.py:299
  4.0 0.0 copy-start.2
  4.0 0.0 copy-start.3
  4.0 0.0 copy-start.4
  4.0 0.0 copy-start.1
  4.0 4.3 %all-to-all-start = ((bf16[4,192,1024]{2,1,0:T(8,128)(2,1)}), bf16[4,192,1024]{2,1,0:T(8,128)(2,1)S(1)}, u32[]{:S(2)}, u32[]{:S(2)}) async-start(bf16[4,192,1024]{2,1,0:T(8,128)(2,1)} %bitcast.54), calls=%async_computation | async-start | bytes 3145728 | tf_op jit(solution)/shard_map/all_to_all | solution.py:304
  8.3 0.1 reshape.223
  8.4 0.0 copy-done.2
  8.5 0.0 copy-done.3
  8.5 0.0 copy-done.4
  8.5 0.1 select_reduce_fusion.1
  8.6 0.1 add_select_fusion
  8.7 0.1 select_n.82
  8.8 0.0 copy-done.1
  8.8 0.6 reshape.227.gain_ref
  9.4 0.9 fusion.8.vis_ref
  10.4 0.3 convert_reduce_fusion
  10.7 1.0 fusion.10
  11.7 1.0 pad_maximum_fusion
  12.7 14.7 %all-to-all-done = bf16[4,192,1024]{2,1,0:T(8,128)(2,1)S(1)} async-done(((bf16[4,192,1024]{2,1,0:T(8,128)(2,1)}), bf16[4,192,1024]{2,1,0:T(8,128)(2,1)S(1)}, u32[]{:S(2)}, u32[]{:S(2)}) %all-to-all-start) | async-done | bytes 1572896 | tf_op jit(solution)/shard_map/all_to_all | solution.py:304
  27.4 2.0 fusion.3.x_ref
  29.4 203.8 %shard_map.91 = bf16[512,1024]{1,0:T(8,128)(2,1)} custom-call(bf16[512,1024]{1,0:T(8,128)(2,1)} %fusion.3.x_ref, f32[8,1024]{1,0:T(8,128)} %reshape.227.gain_ref, bf16[2048,512]{1,0:T(8,128)(2,1)} %q_ref.1, bf16[2048,128]{1,0:T(8,128)(2,1)} %k_ref.1, bf16[2048,128]{1,0:T(8,128)(2,1)} %v_ref.1, bf16[512,2048]{1,0:T(8,128)(2,1)} %o_ref.1, ...), custom_call_target="tpu_custom_call" | custom-call | tf_op jit(solution)/shard_map/pallas_call | solution.py:348
  233.2 2.3 copy.11
  (10 shorter events, 0.1 us)
Async XLA Ops:
  0.0 1.4 copy-start
  4.0 4.4 %copy-start.2 = (s32[512]{0:T(512)S(1)}, s32[512]{0:T(512)}, u32[]{:S(2)}) copy-start(s32[512]{0:T(512)} %param.17) | copy-start | bytes 6148
  4.0 4.5 %copy-start.3 = (s32[64]{0:T(128)S(1)}, s32[64]{0:T(128)}, u32[]{:S(2)}) copy-start(s32[64]{0:T(128)} %param.15) | copy-start | bytes 772
  4.0 4.5 %copy-start.4 = (s32[64,2]{0,1:T(2,128)S(1)}, s32[64,2]{0,1:T(2,128)}, u32[]{:S(2)}) copy-start(s32[64,2]{0,1:T(2,128)} %param.16) | copy-start | bytes 1540
  4.0 4.8 %copy-start.1 = (f32[8192]{0:T(1024)S(1)}, f32[8192]{0:T(1024)}, u32[]{:S(2)}) copy-start(f32[8192]{0:T(1024)} %param.10) | copy-start | bytes 98308
  4.0 23.4 %all-to-all-start = ((bf16[4,192,1024]{2,1,0:T(8,128)(2,1)}), bf16[4,192,1024]{2,1,0:T(8,128)(2,1)S(1)}, u32[]{:S(2)}, u32[]{:S(2)}) async-start(bf16[4,192,1024]{2,1,0:T(8,128)(2,1)} %bitcast.54), calls=%async_computation | async-start | bytes 3145728 | tf_op jit(solution)/shard_map/all_to_all | solution.py:304

commit v2 on v1

--- a/solution.py
+++ b/solution.py
@@ -2,6 +2,7 @@
 
 import jax
 import jax.numpy as jnp
+import numpy as np
 from jax import lax
 from jax.experimental import pallas as pl
 from jax.experimental.pallas import tpu as pltpu
@@ -14,56 +15,111 @@
 MESH = pl.DeviceIdType.MESH
 
 
-def row_mask(ids):
-    pair_of = ids // 3
-    role_of = ids % 3
-    steps_a = jnp.arange(ids.shape[0])
-    causal = steps_a[None, :] <= steps_a[:, None]
-    same = pair_of[:, None] == pair_of[None, :]
-    hidden_pair = (role_of[:, None] == 2) & (role_of[None, :] == 1)
-    return causal & same & jnp.logical_not(hidden_pair)
-
-
 def ring_member(place, count):
     place = lax.rem(place + 2 * count, count)
     return jnp.where(place < count // 2, 2 * place, 2 * (count - 1 - place) + 1)
 
 
+def pieces_of_output(n_mp, width, chunk):
+    if width != 2 * chunk:
+        return 1
+    order = list(range(0, n_mp, 2)) + list(range(1, n_mp, 2))[::-1]
+    apart = all(order[p - 1] // 2 != order[(p + 1) % n_mp] // 2 for p in range(n_mp))
+    return 2 if apart else 1
+
+
 def kernel(
     n_dp, n_mp,
-    x_ref, gain_ref, q_ref, k_ref, v_ref, o_ref, cos_ref, sin_ref, vis_ref,
+    map_ref, tok_ref, gain_ref, q_ref, k_ref, v_ref, o_ref, ids_ref, freq_ref,
     out_ref,
-    xg, wq, wk, wv, wo, acc, attn, sums, terms,
-    own_sem, w_send, w_recv, x_send, x_recv, s_send, s_recv,
+    xin, xg, wq, wk, wv, wo, acc, square, attn, sums, terms, cos_ref, sin_ref, vis_ref,
+    own_sem, t_send, t_recv, w_send, w_recv, x_send, x_recv, s_send, s_recv,
 ):
     me_dp = lax.axis_index("dp")
     me_mp = lax.axis_index("mp")
-    place = jnp.where(lax.rem(me_mp, 2) == 0, me_mp // 2, n_mp - 1 - me_mp // 2)
+
+    def place_of(g):
+        return jnp.where(lax.rem(g, 2) == 0, g // 2, n_mp - 1 - g // 2)
+
+    place = place_of(me_mp)
     sides = (ring_member(place + 1, n_mp), ring_member(place - 1, n_mp))
     groups = n_dp // 2
     core = lax.rem(me_dp, 2)
     partner = me_dp + 1 - 2 * core
     others = [lax.rem(me_dp + 2 * j, n_dp) for j in range(1, groups)]
-    tokens, chunk = x_ref.shape
+    tokens, chunk = out_ref.shape
     half = tokens // 2
     piece = half // PIECES
+    block = tok_ref.shape[0] // n_dp
+    width = o_ref.shape[1]
+    n_out = pieces_of_output(n_mp, width, chunk)
 
     barrier = pltpu.get_barrier_semaphore()
     for side in sides:
         pl.semaphore_signal(barrier, inc=1, device_id={"mp": side}, device_id_type=MESH)
-    for peer in [partner] + others:
+    for j in range(1, n_dp):
+        peer = lax.rem(me_dp + j, n_dp)
         pl.semaphore_signal(barrier, inc=1, device_id={"dp": peer}, device_id_type=MESH)
-    pl.semaphore_wait(barrier, 2 + 1 + len(others))
+    pl.semaphore_wait(barrier, 2 + n_dp - 1)
+
+    def token_rows(owner):
+        return pl.ds(pl.multiple_of(owner * block, 16), block)
+
+    def token_copy(j):
+        peer = lax.rem(me_dp + j, n_dp)
+        return pltpu.make_async_remote_copy(
+            src_ref=tok_ref.at[token_rows(peer), :],
+            dst_ref=xin.at[token_rows(me_dp), :],
+            send_sem=t_send.at[j - 1],
+            recv_sem=t_recv.at[me_dp],
+            device_id={"dp": peer},
+            device_id_type=MESH,
+        )
+
+    def token_arrival(j):
+        peer = lax.rem(me_dp + j, n_dp)
+        return pltpu.make_async_remote_copy(
+            src_ref=tok_ref.at[token_rows(peer), :],
+            dst_ref=xin.at[token_rows(peer), :],
+            send_sem=t_send.at[j - 1],
+            recv_sem=t_recv.at[peer],
+            device_id={"dp": peer},
+            device_id_type=MESH,
+        )
+
+    own_tokens = pltpu.make_async_copy(
+        tok_ref.at[token_rows(me_dp), :], xin.at[token_rows(me_dp), :], own_sem.at[4]
+    )
+    for j in range(1, n_dp):
+        token_copy(j).start()
+    own_tokens.start()
+
+    def hop_of(g):
+        gap = lax.rem(place_of(g) - place + n_mp, n_mp)
+        gap = jnp.where(gap == 0, n_mp, gap)
+        return jnp.minimum(gap, jnp.where(gap == n_mp, n_mp, n_mp - gap))
+
+    def out_columns(which, owner):
+        if n_out == 1:
+            return owner * 0
+        later = (hop_of(2 * owner + 1) < hop_of(2 * owner)).astype(jnp.int32)
+        return chunk * (later if which == 3 else 1 - later)
 
     def part(which, owner):
-        if which == 3:
-            width = o_ref.shape[1]
-            return wo.at[:, pl.ds(pl.multiple_of(owner * width, 128), width)]
+        if which >= 3:
+            start = owner * width + out_columns(which, owner)
+            return wo.at[:, pl.ds(pl.multiple_of(start, 128), width // n_out)]
         full = (wq, wk, wv)[which]
         depth = q_ref.shape[0]
         return full.at[pl.ds(pl.multiple_of(owner * depth, 16), depth), :]
 
-    shards = (q_ref, k_ref, v_ref, o_ref)
+    def shard(which):
+        if which >= 3:
+            start = out_columns(which, me_dp)
+            return o_ref.at[:, pl.ds(pl.multiple_of(start, 128), width // n_out)]
+        return (q_ref, k_ref, v_ref)[which]
+
+    kinds = 3 + n_out
 
     def weight_copy(which, owner, source, slot, peer):
         return pltpu.make_async_remote_copy(
@@ -103,21 +159,68 @@
             device_id_type=MESH,
         )
 
-    own_x = pltpu.make_async_copy(x_ref, xg.at[me_mp], own_sem.at[4])
-    own_x.start()
     owns = [
-        pltpu.make_async_copy(shards[w], part(w, me_dp), own_sem.at[w]) for w in range(4)
+        pltpu.make_async_copy(
+            (q_ref, k_ref, v_ref)[w],
+            part(w, me_dp),
+            own_sem.at[w],
+        )
+        for w in range(3)
     ]
-    for w in range(4):
+    owns.append(
+        pltpu.make_async_copy(
+            o_ref,
+            wo.at[:, pl.ds(pl.multiple_of(me_dp * width, 128), width)],
+            own_sem.at[3],
+        )
+    )
+    for w in range(kinds):
         for j, peer in enumerate(others):
-            weight_copy(w, me_dp, shards[w], 1 + j, peer).start()
-    own_x.wait()
+            weight_copy(w, me_dp, shard(w), 1 + j, peer).start()
+    for w in range(3):
+        owns[w].start()
+        weight_copy(w, me_dp, shard(w), 0, partner).start()
+
+    def tables(r, carry):
+        rows = pl.ds(pl.multiple_of(r * ROW_TOKENS, ROW_TOKENS), ROW_TOKENS)
+        ids_j = jnp.broadcast_to(ids_ref[pl.ds(r, 1), :], (ROW_TOKENS, ROW_TOKENS)).astype(
+            jnp.float32
+        )
+        ids_i = jnp.transpose(ids_j)
+        pair_i = jnp.floor((ids_i + 0.5) * (1.0 / 3.0))
+        pair_j = jnp.floor((ids_j + 0.5) * (1.0 / 3.0))
+        at_i = lax.broadcasted_iota(jnp.int32, (ROW_TOKENS, ROW_TOKENS), 0)
+        at_j = lax.broadcasted_iota(jnp.int32, (ROW_TOKENS, ROW_TOKENS), 1)
+        hidden = (ids_i - 3.0 * pair_i == 2.0) & (ids_j - 3.0 * pair_j == 1.0)
+        seen = jnp.where((at_j <= at_i) & (pair_i == pair_j), 1.0, 0.0)
+        seen = jnp.where(hidden, 0.0, seen)
+        vis_ref[rows, :] = seen
+        angle = (jnp.sum(seen, axis=1, keepdims=True) - 1.0) * freq_ref[...]
+        lane = lax.broadcasted_iota(jnp.int32, (ROW_TOKENS, HEAD_SIZE), 1)
+        sine = jnp.sin(angle)
+        cos_ref[rows, :] = jnp.cos(angle)
+        sin_ref[rows, :] = jnp.where(lane < HEAD_SIZE // 2, -sine, sine)
+        return carry
+
+    lax.fori_loop(0, tokens // ROW_TOKENS, tables, 0)
+    acc[...] = jnp.zeros_like(acc)
+    square[...] = jnp.zeros_like(square)
+
+    own_tokens.wait()
+    for j in range(1, n_dp):
+        token_arrival(j).wait_recv()
     for sub in range(PIECES):
         for way in range(2):
+            start = way * half + sub * piece
+            at = lax.broadcasted_iota(jnp.int32, (piece, n_dp * block), 0) + start
+            put = jnp.where(at == map_ref[...], 1.0, 0.0).astype(jnp.bfloat16)
+            xg[me_mp, start:start + piece, :] = jnp.dot(
+                put, xin[...], preferred_element_type=jnp.float32
+            ).astype(jnp.bfloat16)
             x_copy(0, way, sub).start()
-    for w in range(4):
-        owns[w].start()
-        weight_copy(w, me_dp, shards[w], 0, partner).start()
+    owns[3].start()
+    for w in range(3, kinds):
+        weight_copy(w, me_dp, shard(w), 0, partner).start()
 
     def pass_weight(w):
         for j in range(1, groups):
@@ -126,17 +229,60 @@
             weight_copy(w, owner, part(w, owner), groups + j - 1, partner).start()
 
     def weight_done(w):
-        owns[w].wait()
         for i in range(groups):
             owner = lax.rem(partner + 2 * i, n_dp)
             weight_copy(w, owner, part(w, owner), 0, partner).wait_recv()
 
+    q_width = wq.shape[1]
+    k_width = wk.shape[1]
+
+    def project(way, g):
+        halves = pl.ds(pl.multiple_of(way * half, 16), half)
+        wide = xg[g, halves, :].astype(jnp.float32)
+        square[halves, :] += jnp.sum(wide * wide, axis=1, keepdims=True)
+        columns = pl.ds(pl.multiple_of(g * chunk, 128), chunk)
+        scaled = (wide * gain_ref[:, columns]).astype(jnp.bfloat16)
+        rows = pl.ds(pl.multiple_of(g * chunk, 16), chunk)
+        acc[halves, 0:q_width] += jnp.dot(
+            scaled, wq[rows, :], preferred_element_type=jnp.float32
+        )
+        acc[halves, q_width:q_width + k_width] += jnp.dot(
+            scaled, wk[rows, :], preferred_element_type=jnp.float32
+        )
+        acc[halves, q_width + k_width:] += jnp.dot(
+            scaled, wv[rows, :], preferred_element_type=jnp.float32
+        )
+
+    def project_step(hop, near):
+        def one(way, carry):
+            g = ring_member(place + jnp.where(way == 0, -hop, hop), n_mp)
+            is_near = (g * chunk) // (2 * q_ref.shape[0]) == me_dp // 2
+
+            @pl.when(is_near == near)
+            def _():
+                project(way, g)
+
+            return carry
+
+        lax.fori_loop(0, 2, one, 0)
+
+    for w in range(3):
+        owns[w].wait()
+        owner = partner
+        weight_copy(w, owner, part(w, owner), 0, partner).wait_recv()
+
     def gather_step(step, carry):
+        project_step(step, True)
         for sub in range(PIECES):
             for way in range(2):
                 x_arrival(step, way, sub).wait_recv()
                 x_copy(step + 1, way, sub).start()
         return carry
+
+    def weight_rest(w):
+        for i in range(1, groups):
+            owner = lax.rem(partner + 2 * i, n_dp)
+            weight_copy(w, owner, part(w, owner), 0, partner).wait_recv()
 
     late = max(n_mp - 3, 0)
     lax.fori_loop(0, late, gather_step, 0)
@@ -144,32 +290,25 @@
     lax.fori_loop(late, n_mp - 2, gather_step, 0)
     pass_weight(1)
     pass_weight(2)
+    project_step(n_mp - 2, True)
+    for w in range(3):
+        weight_rest(w)
+
+    def project_far(hop, carry):
+        project_step(hop, False)
+        return carry
+
+    lax.fori_loop(0, n_mp - 1, project_far, 0)
     for sub in range(PIECES):
         for way in range(2):
             x_arrival(n_mp - 2, way, sub).wait_recv()
-    for w in range(3):
-        weight_done(w)
-
-    q_width = wq.shape[1]
-    k_width = wk.shape[1]
-    acc[...] = jnp.zeros_like(acc)
-
-    def project(g, squares):
-        wide = xg[g].astype(jnp.float32)
-        squares = squares + jnp.sum(wide * wide, axis=1, keepdims=True)
-        scaled = (wide * gain_ref[pl.ds(g, 1), :]).astype(jnp.bfloat16)
-        rows = pl.ds(pl.multiple_of(g * chunk, 16), chunk)
-        acc[:, 0:q_width] += jnp.dot(scaled, wq[rows, :], preferred_element_type=jnp.float32)
-        acc[:, q_width:q_width + k_width] += jnp.dot(
-            scaled, wk[rows, :], preferred_element_type=jnp.float32
-        )
-        acc[:, q_width + k_width:] += jnp.dot(
-            scaled, wv[rows, :], preferred_element_type=jnp.float32
-        )
-        return squares
-
-    squares = lax.fori_loop(0, n_mp, project, jnp.zeros((tokens, 1), jnp.float32))
-    acc[...] = acc[...] * lax.rsqrt(squares / (n_mp * chunk) + 1e-05)
+
+    def project_last(way, carry):
+        project(way, ring_member(place + jnp.where(way == 0, 1 - n_mp, n_mp - 1), n_mp))
+        return carry
+
+    lax.fori_loop(0, 2, project_last, 0)
+    acc[...] = acc[...] * lax.rsqrt(square[...] / (n_mp * chunk) + 1e-05)
 
     def turn(u, cosine, sine):
         return (u * cosine + pltpu.roll(u, HEAD_SIZE // 2, 1) * sine).astype(jnp.bfloat16)
@@ -178,7 +317,7 @@
         rows = pl.ds(pl.multiple_of(r * ROW_TOKENS, ROW_TOKENS), ROW_TOKENS)
         cosine = cos_ref[rows, :]
         sine = sin_ref[rows, :]
-        seen = vis_ref[rows, :] > 0
+        seen = vis_ref[rows, :] > 0.5
         for kv in range(k_width // HEAD_SIZE):
             at_k = q_width + kv * HEAD_SIZE
             key = turn(acc[rows, at_k:at_k + HEAD_SIZE], cosine, sine)
@@ -198,6 +337,7 @@
         return carry
 
     lax.fori_loop(0, tokens // ROW_TOKENS, attend, 0)
+    owns[3].wait()
     pass_weight(3)
     weight_done(3)
 
@@ -230,6 +370,10 @@
             sums[way, 0, rows, :] = terms[way, rows, :].astype(jnp.bfloat16)
             sum_copy(0, way, sub).start()
 
+    for w in range(4, kinds):
+        pass_weight(w)
+        weight_done(w)
+
     def scatter_step(step, carry):
         make_terms(step + 2)
         for sub in range(PIECES):
@@ -259,9 +403,11 @@
         return carry
 
     lax.fori_loop(0, n_mp - 1, drain, 0)
-    for w in range(4):
+    for j in range(1, n_dp):
+        token_copy(j).wait_send()
+    for w in range(kinds):
         for i in range(2 * groups - 1):
-            weight_copy(w, me_dp, shards[w], i, partner).wait_send()
+            weight_copy(w, me_dp, shard(w), i, partner).wait_send()
 
 
 def local(
@@ -301,13 +447,6 @@
         pair_tokens.reshape(pairs_dev * pair_cap, width_local),
         preferred_element_type=jnp.float32,
     ).astype(jnp.bfloat16)
-    incoming = lax.all_to_all(
-        outgoing.reshape(dp_count, most_sent * pair_cap, width_local),
-        "dp",
-        split_axis=0,
-        concat_axis=0,
-        tiled=True,
-    )
     length = pair_span[:, 1] - pair_span[:, 0]
     source = jnp.arange(all_pairs, dtype=jnp.int32) // pairs_dev
     first = (pair_row % rows_dev) * ROW_TOKENS + pair_span[:, 0]
@@ -319,24 +458,9 @@
     placement_map = jnp.where(
         slots[None, :] < length_of[:, None], first_of[:, None] + slots[None, :], tok_dev
     ).reshape(-1)
-    put = (jnp.arange(tok_dev)[:, None] == placement_map[None, :]).astype(jnp.bfloat16)
-    packed_local = jnp.dot(
-        put,
-        incoming.reshape(sent * pair_cap, width_local),
-        preferred_element_type=jnp.float32,
-    ).astype(jnp.bfloat16)
-
-    ids_rows = block_ids.reshape(rows_dev, ROW_TOKENS)
-    visible = jax.vmap(row_mask)(ids_rows)
-    token_position = (jnp.sum(visible.astype(jnp.int32), axis=2) - 1).reshape(tok_dev)
     half = HEAD_SIZE // 2
-    freq = 500000.0 ** (-(jnp.arange(half, dtype=jnp.float32) * 2.0 / HEAD_SIZE))
-    angle = token_position.astype(jnp.float32)[:, None] * freq[None, :]
-    cosine = jnp.cos(angle)
-    sine = jnp.sin(angle)
-    cosine = jnp.concatenate([cosine, cosine], axis=1)
-    sine = jnp.concatenate([-sine, sine], axis=1)
-    seen = visible.astype(jnp.int32).reshape(tok_dev, ROW_TOKENS)
+    freq = 500000.0 ** (-(np.arange(half, dtype=np.float32) * 2.0 / HEAD_SIZE))
+    freq = np.concatenate([freq, freq])[None, :].astype(np.float32)
 
     q_width = q_weight.shape[1]
     k_width = k_weight.shape[1]
@@ -348,21 +472,28 @@
     return pl.pallas_call(
         functools.partial(kernel, dp_count, mp_count),
         out_shape=jax.ShapeDtypeStruct((tok_dev, width_local), bf16),
-        in_specs=[anyspace, vmem, anyspace, anyspace, anyspace, anyspace, vmem, vmem, vmem],
+        in_specs=[vmem, anyspace, vmem, anyspace, anyspace, anyspace, anyspace, vmem, vmem],
         out_specs=vmem,
         scratch_shapes=[
+            pltpu.VMEM((sent * pair_cap, width_local), bf16),
             pltpu.VMEM((mp_count, tok_dev, width_local), bf16),
             pltpu.VMEM((width, q_width), bf16),
             pltpu.VMEM((width, k_width), bf16),
             pltpu.VMEM((width, k_width), bf16),
             pltpu.VMEM((o_weight.shape[0], width), bf16),
             pltpu.VMEM((tok_dev, q_width + 2 * k_width), jnp.float32),
+            pltpu.VMEM((tok_dev, 1), jnp.float32),
             pltpu.VMEM((tok_dev, q_width), bf16),
             pltpu.VMEM((2, mp_count, tok_dev // 2, width_local), bf16),
             pltpu.VMEM((2, tok_dev // 2, width_local), jnp.float32),
+            pltpu.VMEM((tok_dev, HEAD_SIZE), jnp.float32),
+            pltpu.VMEM((tok_dev, HEAD_SIZE), jnp.float32),
+            pltpu.VMEM((tok_dev, ROW_TOKENS), jnp.float32),
             pltpu.SemaphoreType.DMA((5,)),
-            pltpu.SemaphoreType.DMA((4, far)),
-            pltpu.SemaphoreType.DMA((4, dp_count)),
+            pltpu.SemaphoreType.DMA((far,)),
+            pltpu.SemaphoreType.DMA((dp_count,)),
+            pltpu.SemaphoreType.DMA((5, far)),
+            pltpu.SemaphoreType.DMA((5, dp_count)),
             pltpu.SemaphoreType.DMA((2, PIECES, mp_count - 1)),
             pltpu.SemaphoreType.DMA((2, PIECES, mp_count - 1)),
             pltpu.SemaphoreType.DMA((2, PIECES, mp_count - 1)),
@@ -372,15 +503,15 @@
             collective_id=0, has_side_effects=True, vmem_limit_bytes=60 * 1024 * 1024
         ),
     )(
-        packed_local,
-        norm_gain.reshape(mp_count, width_local),
+        placement_map[None, :],
+        outgoing,
+        norm_gain[None, :],
         q_weight,
         k_weight,
         value_weight,
         o_weight,
-        cosine,
-        sine,
-        seen,
+        block_ids.reshape(rows_dev, ROW_TOKENS),
+        jnp.asarray(freq),
     )
 
 

time: 237 us -> 219 us (0.924)
  waiting for transfers between devices: 14.7 us -> 0 us
  Pallas kernels: 204 us -> 209 us
  starting transfers between devices: 4.35 us -> 0 us
  other arithmetic: 4.65 us -> 1.93 us
    all_to_all x1 -> x0, waiting for transfers between devices: 14.7 us -> none  [local(): lax.all_to_all(outgoing.reshape(dp_count, most_sent * pair_cap, width_loc...]
    pallas_call x1, Pallas kernels: 204 us -> 209 us  [local(): pl.pallas_call(functools.partial(kernel, dp_count, mp_count), out_shape=j...]
    all_to_all x1 -> x0, starting transfers between devices: 4.35 us -> none  [local(): lax.all_to_all(outgoing.reshape(dp_count, most_sent * pair_cap, width_loc...]
  transfers between devices with their start and end apart: 1 -> 0, of which waited for: 1 -> 0; matrix products, arithmetic and copies ran while one was open for 2% -> 0% of each run, Pallas kernels for 0% -> 0%
where the time goes in v2:
time: 219 us; the launch traced here: 218 us
  Pallas kernels  209 us (95%)
  local copies, waits for them, and re-layouts  4.58 us (2%)
  matrix products  2.54 us (1%)
    pallas_call x1, Pallas kernels, local(): pl.pallas_call(functools.partial(kernel, dp_count, mp_count), out_shape=j...  209 us

profile of v2, /device:TPU:17, one launch (start us, length us, event | category | flops | bytes accessed | tf_op | source)
XLA Modules:
  0.0 217.7 jit_solution(9683579626736145542)
XLA Ops:
  0.0 0.0 copy-start
  0.0 1.4 copy-done
  1.4 0.7 broadcast_compare_fusion
  2.1 0.1 eq.50
  2.2 0.2 convert_reduce_fusion
  2.4 0.1 reshape.136
  2.5 0.8 fusion.7
  3.3 0.1 select_reduce_fusion.1
  3.4 0.1 add_select_fusion
  3.4 0.7 select_n.51.map_ref
  4.1 0.1 iota_add_fusion
  4.2 0.1 add.81
  4.3 2.5 %fusion.1.tok_ref = bf16[768,1024]{1,0:T(8,128)(2,1)} fusion(bf16[768,1024]{1,0:T(8,128)(2,1)S(1)} %bitcast.11, s32[768]{0:T(1024)S(1)} %add.81), kind=kOutput, calls=%fused_computation.2 | convolution fusion | flops 1209335808 | bytes 3148800 | tf_op jit(solution)/shard_map/dot_general | solution.py:445
  6.8 208.6 %shard_map.100 = bf16[512,1024]{1,0:T(8,128)(2,1)} custom-call(s32[1,768]{1,0:T(1,128)} %select_n.51.map_ref, bf16[768,1024]{1,0:T(8,128)(2,1)} %fusion.1.tok_ref, f32[1,8192]{1,0:T(1,128)} %bitcast.12, bf16[2048,512]{1,0:T(8,128)(2,1)} %q_ref.1, bf16[2048,128]{1,0:T(8,128)(2,1)} %k_ref.1, bf16[2048,128]{1,0:T(8,128)(2,1)} %v_ref.1, ...), custom_call_target="tpu_custom_call" | custom-call | tf_op jit(solution)/shard_map/pallas_call | solution.py:472
  215.4 2.3 %copy.12 = bf16[512,1024]{1,0:T(8,128)(2,1)} copy(bf16[512,1024]{1,0:T(8,128)(2,1)} %shard_map.100) | data formatting | bytes 2097152
  (2 shorter events, 0.0 us)
Async XLA Ops:
  0.0 1.4 copy-start

commit v3 on v2

--- a/solution.py
+++ b/solution.py
@@ -12,6 +12,7 @@
 ROW_TOKENS = 128
 QUERY_PER_KV = 4
 PIECES = 2
+SLICES = 4
 MESH = pl.DeviceIdType.MESH
 
 
@@ -32,7 +33,7 @@
     n_dp, n_mp,
     map_ref, tok_ref, gain_ref, q_ref, k_ref, v_ref, o_ref, ids_ref, freq_ref,
     out_ref,
-    xin, xg, wq, wk, wv, wo, acc, square, attn, sums, terms, cos_ref, sin_ref, vis_ref,
+    xin, xg, wq, wk, wv, wo, acc, square, attn, sums, terms, cos_ref, sin_ref, vis_ref, put_ref,
     own_sem, t_send, t_recv, w_send, w_recv, x_send, x_recv, s_send, s_recv,
 ):
     me_dp = lax.axis_index("dp")
@@ -65,24 +66,29 @@
     def token_rows(owner):
         return pl.ds(pl.multiple_of(owner * block, 16), block)
 
-    def token_copy(j):
+    slice_width = chunk // SLICES
+
+    def token_slice(sub):
+        return pl.ds(sub * slice_width, slice_width)
+
+    def token_copy(j, sub):
         peer = lax.rem(me_dp + j, n_dp)
         return pltpu.make_async_remote_copy(
-            src_ref=tok_ref.at[token_rows(peer), :],
-            dst_ref=xin.at[token_rows(me_dp), :],
-            send_sem=t_send.at[j - 1],
-            recv_sem=t_recv.at[me_dp],
+            src_ref=tok_ref.at[token_rows(peer), token_slice(sub)],
+            dst_ref=xin.at[token_rows(me_dp), token_slice(sub)],
+            send_sem=t_send.at[sub, j - 1],
+            recv_sem=t_recv.at[sub, me_dp],
             device_id={"dp": peer},
             device_id_type=MESH,
         )
 
-    def token_arrival(j):
+    def token_arrival(j, sub):
         peer = lax.rem(me_dp + j, n_dp)
         return pltpu.make_async_remote_copy(
-            src_ref=tok_ref.at[token_rows(peer), :],
-            dst_ref=xin.at[token_rows(peer), :],
-            send_sem=t_send.at[j - 1],
-            recv_sem=t_recv.at[peer],
+            src_ref=tok_ref.at[token_rows(peer), token_slice(sub)],
+            dst_ref=xin.at[token_rows(peer), token_slice(sub)],
+            send_sem=t_send.at[sub, j - 1],
+            recv_sem=t_recv.at[sub, peer],
             device_id={"dp": peer},
             device_id_type=MESH,
         )
@@ -90,8 +96,9 @@
     own_tokens = pltpu.make_async_copy(
         tok_ref.at[token_rows(me_dp), :], xin.at[token_rows(me_dp), :], own_sem.at[4]
     )
-    for j in range(1, n_dp):
-        token_copy(j).start()
+    for sub in range(SLICES):
+        for j in range(1, n_dp):
+            token_copy(j, sub).start()
     own_tokens.start()
 
     def hop_of(g):
@@ -134,8 +141,7 @@
     def x_copy(step, way, sub):
         sign = -1 if way == 0 else 1
         chunk_of = ring_member(place + sign * step, n_mp)
-        rows = pl.ds(way * half + sub * piece, piece)
-        ref = xg.at[chunk_of, rows, :]
+        ref = xg.at[chunk_of, pl.ds(way * half, half), token_slice(sub)]
         return pltpu.make_async_remote_copy(
             src_ref=ref,
             dst_ref=ref,
@@ -148,8 +154,7 @@
     def x_arrival(step, way, sub):
         sign = -1 if way == 0 else 1
         chunk_of = ring_member(place + sign * (step + 1), n_mp)
-        rows = pl.ds(way * half + sub * piece, piece)
-        ref = xg.at[chunk_of, rows, :]
+        ref = xg.at[chunk_of, pl.ds(way * half, half), token_slice(sub)]
         return pltpu.make_async_remote_copy(
             src_ref=ref,
             dst_ref=ref,
@@ -174,9 +179,24 @@
             own_sem.at[3],
         )
     )
-    for w in range(kinds):
+    def second_chunk(owner):
+        return (owner * width + out_columns(4, owner)) // chunk
+
+    def second_stage(owner):
+        hop = hop_of(second_chunk(owner))
+        return jnp.where(hop == n_mp, 2, jnp.where(hop > 2, 1, 0))
+
+    held = second_stage(me_dp) == 2
+
+    def send_second():
+        for j, peer in enumerate(others):
+            weight_copy(4, me_dp, shard(4), 1 + j, peer).start()
+
+    for w in range(min(kinds, 4)):
         for j, peer in enumerate(others):
             weight_copy(w, me_dp, shard(w), 1 + j, peer).start()
+    if kinds == 5:
+        pl.when(jnp.logical_not(held))(send_second)
     for w in range(3):
         owns[w].start()
         weight_copy(w, me_dp, shard(w), 0, partner).start()
@@ -207,16 +227,16 @@
     square[...] = jnp.zeros_like(square)
 
     own_tokens.wait()
-    for j in range(1, n_dp):
-        token_arrival(j).wait_recv()
-    for sub in range(PIECES):
+    at = lax.broadcasted_iota(jnp.int32, (tokens, n_dp * block), 0)
+    put_ref[...] = jnp.where(at == map_ref[...], 1.0, 0.0).astype(jnp.bfloat16)
+    for sub in range(SLICES):
+        for j in range(1, n_dp):
+            token_arrival(j, sub).wait_recv()
+        columns = slice(sub * slice_width, (sub + 1) * slice_width)
+        xg[me_mp, :, columns] = jnp.dot(
+            put_ref[...], xin[:, columns], preferred_element_type=jnp.float32
+        ).astype(jnp.bfloat16)
         for way in range(2):
-            start = way * half + sub * piece
-            at = lax.broadcasted_iota(jnp.int32, (piece, n_dp * block), 0) + start
-            put = jnp.where(at == map_ref[...], 1.0, 0.0).astype(jnp.bfloat16)
-            xg[me_mp, start:start + piece, :] = jnp.dot(
-                put, xin[...], preferred_element_type=jnp.float32
-            ).astype(jnp.bfloat16)
             x_copy(0, way, sub).start()
     owns[3].start()
     for w in range(3, kinds):
@@ -273,7 +293,7 @@
 
     def gather_step(step, carry):
         project_step(step, True)
-        for sub in range(PIECES):
+        for sub in range(SLICES):
             for way in range(2):
                 x_arrival(step, way, sub).wait_recv()
                 x_copy(step + 1, way, sub).start()
@@ -299,7 +319,7 @@
         return carry
 
     lax.fori_loop(0, n_mp - 1, project_far, 0)
-    for sub in range(PIECES):
+    for sub in range(SLICES):
         for way in range(2):
             x_arrival(n_mp - 2, way, sub).wait_recv()
 
@@ -337,6 +357,8 @@
         return carry
 
     lax.fori_loop(0, tokens // ROW_TOKENS, attend, 0)
+    if kinds == 5:
+        pl.when(held)(send_second)
     owns[3].wait()
     pass_weight(3)
     weight_done(3)
@@ -370,11 +392,31 @@
             sums[way, 0, rows, :] = terms[way, rows, :].astype(jnp.bfloat16)
             sum_copy(0, way, sub).start()
 
-    for w in range(4, kinds):
-        pass_weight(w)
-        weight_done(w)
+    def second_pieces(stage):
+        if kinds < 5:
+            return
+        for j in range(1, groups):
+            owner = lax.rem(me_dp + n_dp - 2 * j, n_dp)
+
+            @pl.when(second_stage(owner) == stage)
+            def _():
+                weight_copy(4, owner, part(4, owner), 0, partner).wait_recv()
+                weight_copy(4, owner, part(4, owner), groups + j - 1, partner).start()
+
+        for i in range(groups):
+            owner = lax.rem(partner + 2 * i, n_dp)
+
+            @pl.when(second_stage(owner) == stage)
+            def _():
+                weight_copy(4, owner, part(4, owner), 0, partner).wait_recv()
+
+    second_pieces(0)
 
     def scatter_step(step, carry):
+        @pl.when(step == 1)
+        def _():
+            second_pieces(1)
+
         make_terms(step + 2)
         for sub in range(PIECES):
             for way in range(2):
@@ -386,6 +428,7 @@
         return carry
 
     lax.fori_loop(0, n_mp - 2, scatter_step, 0)
+    second_pieces(2)
     make_terms(n_mp)
     for sub in range(PIECES):
         for way in range(2):
@@ -396,15 +439,17 @@
             out_ref[start:start + piece, :] = total.astype(jnp.bfloat16)
 
     def drain(step, carry):
-        for sub in range(PIECES):
-            for way in range(2):
+        for way in range(2):
+            for sub in range(SLICES):
                 x_copy(step, way, sub).wait_send()
+            for sub in range(PIECES):
                 sum_copy(step, way, sub).wait_send()
         return carry
 
     lax.fori_loop(0, n_mp - 1, drain, 0)
-    for j in range(1, n_dp):
-        token_copy(j).wait_send()
+    for sub in range(SLICES):
+        for j in range(1, n_dp):
+            token_copy(j, sub).wait_send()
     for w in range(kinds):
         for i in range(2 * groups - 1):
             weight_copy(w, me_dp, shard(w), i, partner).wait_send()
@@ -489,13 +534,14 @@
             pltpu.VMEM((tok_dev, HEAD_SIZE), jnp.float32),
             pltpu.VMEM((tok_dev, HEAD_SIZE), jnp.float32),
             pltpu.VMEM((tok_dev, ROW_TOKENS), jnp.float32),
+            pltpu.VMEM((tok_dev, sent * pair_cap), bf16),
             pltpu.SemaphoreType.DMA((5,)),
-            pltpu.SemaphoreType.DMA((far,)),
-            pltpu.SemaphoreType.DMA((dp_count,)),
+            pltpu.SemaphoreType.DMA((SLICES, far)),
+            pltpu.SemaphoreType.DMA((SLICES, dp_count)),
             pltpu.SemaphoreType.DMA((5, far)),
             pltpu.SemaphoreType.DMA((5, dp_count)),
-            pltpu.SemaphoreType.DMA((2, PIECES, mp_count - 1)),
-            pltpu.SemaphoreType.DMA((2, PIECES, mp_count - 1)),
+            pltpu.SemaphoreType.DMA((2, SLICES, mp_count - 1)),
+            pltpu.SemaphoreType.DMA((2, SLICES, mp_count - 1)),
             pltpu.SemaphoreType.DMA((2, PIECES, mp_count - 1)),
             pltpu.SemaphoreType.DMA((2, PIECES, mp_count - 1)),
         ],

time: 219 us -> 218 us (level)
  no operation moved by 1% of the time
where the time goes in v3:
time: 218 us; the launch traced here: 217 us
  Pallas kernels  208 us (95%)
  local copies, waits for them, and re-layouts  4.58 us (2%)
  matrix products  2.54 us (1%)
    pallas_call x1, Pallas kernels, local(): pl.pallas_call(functools.partial(kernel, dp_count, mp_count), out_shape=j...  208 us

profile of v3, /device:TPU:17, one launch (start us, length us, event | category | flops | bytes accessed | tf_op | source)
XLA Modules:
  0.0 217.3 jit_solution(17657539233362236046)
XLA Ops:
  0.0 0.0 copy-start
  0.0 1.4 copy-done
  1.4 0.7 broadcast_compare_fusion
  2.1 0.1 eq.50
  2.2 0.2 convert_reduce_fusion
  2.4 0.1 reshape.136
  2.5 0.8 fusion.7
  3.3 0.1 select_reduce_fusion.1
  3.4 0.1 add_select_fusion
  3.4 0.7 select_n.51.map_ref
  4.1 0.1 iota_add_fusion
  4.2 0.1 add.81
  4.3 2.5 %fusion.1.tok_ref = bf16[768,1024]{1,0:T(8,128)(2,1)} fusion(bf16[768,1024]{1,0:T(8,128)(2,1)S(1)} %bitcast.11, s32[768]{0:T(1024)S(1)} %add.81), kind=kOutput, calls=%fused_computation.2 | convolution fusion | flops 1209335808 | bytes 3148800 | tf_op jit(solution)/shard_map/dot_general | solution.py:490
  6.8 208.2 %shard_map.100 = bf16[512,1024]{1,0:T(8,128)(2,1)} custom-call(s32[1,768]{1,0:T(1,128)} %select_n.51.map_ref, bf16[768,1024]{1,0:T(8,128)(2,1)} %fusion.1.tok_ref, f32[1,8192]{1,0:T(1,128)} %bitcast.12, bf16[2048,512]{1,0:T(8,128)(2,1)} %q_ref.1, bf16[2048,128]{1,0:T(8,128)(2,1)} %k_ref.1, bf16[2048,128]{1,0:T(8,128)(2,1)} %v_ref.1, ...), custom_call_target="tpu_custom_call" | custom-call | tf_op jit(solution)/shard_map/pallas_call | solution.py:517
  215.0 2.3 %copy.12 = bf16[512,1024]{1,0:T(8,128)(2,1)} copy(bf16[512,1024]{1,0:T(8,128)(2,1)} %shard_map.100) | data formatting | bytes 2097152
  (2 shorter events, 0.0 us)
Async XLA Ops:
  0.0 1.4 copy-start

commit v4 on v3

--- a/solution.py
+++ b/solution.py
@@ -192,11 +192,9 @@
         for j, peer in enumerate(others):
             weight_copy(4, me_dp, shard(4), 1 + j, peer).start()
 
-    for w in range(min(kinds, 4)):
+    for w in range(3):
         for j, peer in enumerate(others):
             weight_copy(w, me_dp, shard(w), 1 + j, peer).start()
-    if kinds == 5:
-        pl.when(jnp.logical_not(held))(send_second)
     for w in range(3):
         owns[w].start()
         weight_copy(w, me_dp, shard(w), 0, partner).start()
@@ -310,6 +308,8 @@
     lax.fori_loop(late, n_mp - 2, gather_step, 0)
     pass_weight(1)
     pass_weight(2)
+    for j, peer in enumerate(others):
+        weight_copy(3, me_dp, shard(3), 1 + j, peer).start()
     project_step(n_mp - 2, True)
     for w in range(3):
         weight_rest(w)
@@ -357,10 +357,10 @@
         return carry
 
     lax.fori_loop(0, tokens // ROW_TOKENS, attend, 0)
-    if kinds == 5:
-        pl.when(held)(send_second)
     owns[3].wait()
     pass_weight(3)
+    if kinds == 5:
+        pl.when(jnp.logical_not(held))(send_second)
     weight_done(3)
 
     def make_terms(hop):
@@ -411,6 +411,8 @@
                 weight_copy(4, owner, part(4, owner), 0, partner).wait_recv()
 
     second_pieces(0)
+    if kinds == 5:
+        pl.when(held)(send_second)
 
     def scatter_step(step, carry):
         @pl.when(step == 1)

time: 218 us -> 219 us (level)
  no operation moved by 1% of the time
where the time goes in v4:
time: 219 us; the launch traced here: 218 us
  Pallas kernels  209 us (95%)
  local copies, waits for them, and re-layouts  4.58 us (2%)
  matrix products  2.54 us (1%)
    pallas_call x1, Pallas kernels, local(): pl.pallas_call(functools.partial(kernel, dp_count, mp_count), out_shape=j...  209 us

profile of v4, /device:TPU:17, one launch (start us, length us, event | category | flops | bytes accessed | tf_op | source)
XLA Modules:
  0.0 218.3 jit_solution(11693069916947798636)
XLA Ops:
  0.0 0.0 copy-start
  0.0 1.4 copy-done
  1.4 0.7 broadcast_compare_fusion
  2.1 0.1 eq.50
  2.2 0.2 convert_reduce_fusion
  2.4 0.1 reshape.136
  2.5 0.8 fusion.7
  3.3 0.1 select_reduce_fusion.1
  3.4 0.1 add_select_fusion
  3.4 0.7 select_n.51.map_ref
  4.1 0.1 iota_add_fusion
  4.2 0.1 add.81
  4.3 2.5 %fusion.1.tok_ref = bf16[768,1024]{1,0:T(8,128)(2,1)} fusion(bf16[768,1024]{1,0:T(8,128)(2,1)S(1)} %bitcast.11, s32[768]{0:T(1024)S(1)} %add.81), kind=kOutput, calls=%fused_computation.2 | convolution fusion | flops 1209335808 | bytes 3148800 | tf_op jit(solution)/shard_map/dot_general | solution.py:492
  6.8 209.2 %shard_map.100 = bf16[512,1024]{1,0:T(8,128)(2,1)} custom-call(s32[1,768]{1,0:T(1,128)} %select_n.51.map_ref, bf16[768,1024]{1,0:T(8,128)(2,1)} %fusion.1.tok_ref, f32[1,8192]{1,0:T(1,128)} %bitcast.12, bf16[2048,512]{1,0:T(8,128)(2,1)} %q_ref.1, bf16[2048,128]{1,0:T(8,128)(2,1)} %k_ref.1, bf16[2048,128]{1,0:T(8,128)(2,1)} %v_ref.1, ...), custom_call_target="tpu_custom_call" | custom-call | tf_op jit(solution)/shard_map/pallas_call | solution.py:519
  216.0 2.3 %copy.12 = bf16[512,1024]{1,0:T(8,128)(2,1)} copy(bf16[512,1024]{1,0:T(8,128)(2,1)} %shard_map.100) | data formatting | bytes 2097152
  (2 shorter events, 0.0 us)
Async XLA Ops:
  0.0 1.4 copy-start
